TPU v7x, 32 devices: a whole 2x2x4 slice. The times are simulated.
32 devices in a mesh: grp: 2 (over y), ka: 4 (over z), ga: 2 (over x), ba: 2 (over core).
Axes of the slice: x: 2, y: 2, z: 4, core: 2. Of those that a mesh axis runs over, the one named last changes fastest.
Arguments:
- coefficients: bfloat16 [2, 2, 16, 512, 9216], P(None, None, ('grp', 'ka'), 'ba', 'ga'), parts along dimension 2, may hold values from -1 to 1
- occupied: int32 [2, 16], P(None, ('grp', 'ka')), parts along dimension 1, may hold values from 64 to 512
- kweights: float32 [16], P(('grp', 'ka')), parts along dimension 0, may hold values from 0.5 to 2
- owner_map: int32 [1024], P('grp'), parts along dimension 0, may hold values from 0 to 7, as said below
- species: int32 [1024], P('grp'), parts along dimension 0, may hold values from 0 to 1
- positions: float32 [3, 1024], P(None, 'grp'), parts along dimension 1, may hold values from 0 to 100
- multipole: float32 [2, 9, 324], replicated, may hold values from -0.3125 to 0.3125
- widths: float32 [2], replicated, may hold values from 0.05 to 0.3
- potential: float32 [2, 442368], P(None, ('grp', 'ga')), parts along dimension 1, may hold values from -0.013671875 to 0.013671875
Outputs:
- density: float32 [2, 2, 1024, 324], P(None, None, ('grp', 'ka', 'ga', 'ba')), parts along dimension 2
- forces: float32 [3, 1024], P(None, ('grp', 'ka', 'ga', 'ba')), parts along dimension 1
There are 2 independent parts, one for each index of `grp`. A program takes and returns all parts, laid end to end along the dimension named above; an argument that names none is the same for every part. Nothing has to cross between parts.
Inputs may be any that keep to these rules, and one draw needn't show every extreme that they name: `owner_map`: within each aligned block of 256 atoms every owner number is named by exactly 32 atoms.
All inputs are finite; a program needn't handle non-finite values.
Results may differ from a plain program's by a relative error of at most 0.0003.
Values sent between devices are 32-bit elements; how exact they have to be, the bound alone decides.
A program may use at most 192 MiB of HBM per device.

v0:
```python
import jax
import jax.numpy as jnp
from jax import lax
from jax.sharding import PartitionSpec as P

NPROJ = 18
SPECIES = 2
NL = 9
GRID = 96
grid_step = 0.0625
highest = lax.Precision.HIGHEST


def harmonics(start_index, length, widths):
    indices = start_index + jnp.arange(length, dtype=jnp.int32)
    planes = [indices % GRID, indices // GRID % GRID, indices // (GRID * GRID)]
    vectors = []
    for plane_index in planes:
        signed = jnp.where(plane_index >= GRID // 2, plane_index - GRID, plane_index)
        vectors.append(grid_step * signed.astype(jnp.float32))
    along_x, along_y, along_z = vectors
    square = along_x * along_x + along_y * along_y + along_z * along_z
    shapes = jnp.stack(
        [
            jnp.ones_like(square),
            along_x,
            along_y,
            along_z,
            along_x * along_y,
            along_y * along_z,
            along_z * along_x,
            along_x * along_x - along_y * along_y,
            3.0 * along_z * along_z - square,
        ]
    )
    damping = jnp.exp(-widths[:, None] * square[None, :])
    form_table = (damping[:, None, :] * shapes[None, :, :]).reshape(SPECIES * NL, length)
    return (form_table, jnp.stack(vectors, axis=1))


def force_block(moments, places, form_table, vectors, pot_piece):
    smooth = jnp.dot(moments, form_table, precision=highest)
    phases = jnp.dot(places, vectors.T, precision=highest)
    wave_term = pot_piece[0][None, :] * jnp.sin(phases) + pot_piece[1][None, :] * jnp.cos(phases)
    return jnp.dot(smooth * wave_term, vectors, precision=highest)


def local_force(moments, places, pot_piece, start_index, widths):
    length = pot_piece.shape[1]
    pieces = 8
    width_block = length // pieces

    def gblock(running, number):
        offset = number * width_block
        form_table, vectors = harmonics(start_index + offset, width_block, widths)
        segment = lax.dynamic_slice_in_dim(pot_piece, offset, width_block, 1)
        return (running + force_block(moments, places, form_table, vectors, segment), None)

    result, unused = lax.scan(
        gblock, jnp.zeros((moments.shape[0], 3), jnp.float32), jnp.arange(pieces, dtype=jnp.int32)
    )
    return result


def shards(
    coefficients, occupied, kweights, owner_map, species, positions, multipole, widths, potential
):
    spin_count, complex_parts, kcount, bcount, columns = coefficients.shape
    atoms_blk = columns // NPROJ
    kgroups = lax.axis_size("ka")
    bgroups = lax.axis_size("ba")
    owners = kgroups * bgroups
    per_owner = atoms_blk // owners
    owner_index = lax.axis_index(("ka", "ba"))
    group_index = lax.axis_index("ga")
    band_index = lax.axis_index("ba") * bcount + jnp.arange(bcount, dtype=jnp.int32)
    band_mask = (band_index[None, None, :] < occupied[:, :, None]).astype(jnp.bfloat16)
    values = coefficients.reshape(spin_count, complex_parts, kcount, bcount, atoms_blk, NPROJ)
    masked = values * band_mask[:, None, :, :, None, None]
    real_part = jnp.einsum(
        "sckbai,sckbaj->skaij", values, masked, preferred_element_type=jnp.float32
    )
    cross_term = jnp.einsum(
        "skbai,skbaj->skaij", values[:, 0], masked[:, 1], preferred_element_type=jnp.float32
    )
    imag_part = cross_term - jnp.swapaxes(cross_term, 3, 4)
    weighted = jnp.stack([real_part, imag_part], axis=1) * kweights[None, None, :, None, None, None]
    density_local = jnp.sum(weighted, axis=2).reshape(
        spin_count, complex_parts, atoms_blk, NPROJ * NPROJ
    )
    ranking = jnp.argsort(owner_map.reshape(-1, atoms_blk), axis=1, stable=True)
    own_ranks = lax.dynamic_slice_in_dim(ranking, owner_index * per_owner, per_owner, 1)
    summed = lax.psum(density_local, ("ka", "ba"))
    own_rows = lax.dynamic_index_in_dim(own_ranks, group_index, 0, keepdims=False)
    own_density = jnp.take(summed, own_rows, axis=2)
    block_count = own_ranks.shape[0]
    atom_ids = jnp.arange(block_count, dtype=jnp.int32)[:, None] * atoms_blk + own_ranks
    own_atoms = lax.dynamic_index_in_dim(atom_ids, group_index, 0, keepdims=False)
    real_total = jnp.sum(own_density[:, 0], axis=0)
    selector = (
        jnp.take(species, own_atoms)[:, None] == jnp.arange(SPECIES, dtype=jnp.int32)[None, :]
    ).astype(jnp.float32)
    moments = jnp.dot(
        real_total, multipole.reshape(SPECIES * NL, NPROJ * NPROJ).T, precision=highest
    ) * jnp.repeat(selector, NL, axis=1)
    gcount = potential.shape[1]
    all_moments = lax.all_gather(moments, "ga", axis=0, tiled=True)
    places = jnp.take(positions, atom_ids.reshape(-1), axis=1).T
    partial_force = local_force(all_moments, places, potential, group_index * gcount, widths)
    summed_force = lax.psum(partial_force, "ga")
    own_force = lax.dynamic_slice_in_dim(summed_force, group_index * per_owner, per_owner, 0)
    return (own_density, own_force.T)


def solution(mesh):
    placed = (
        P(None, None, ("grp", "ka"), "ba", "ga"),
        P(None, ("grp", "ka")),
        P(("grp", "ka")),
        P("grp"),
        P("grp"),
        P(None, "grp"),
        P(),
        P(),
        P(None, ("grp", "ga")),
    )
    return jax.shard_map(
        shards,
        mesh=mesh,
        in_specs=placed,
        out_specs=(
            P(None, None, ("grp", "ka", "ga", "ba"), None),
            P(None, ("grp", "ka", "ga", "ba")),
        ),
        check_vma=False,
    )
```

profile of v0, /device:TPU:0, one launch (start us, length us, event | category | flops | bytes accessed | tf_op | source)
XLA Modules:
  0.0 663.2 jit_solution(12733213700706561287)
XLA Ops:
  8.1 1.3 reshape.503
  10.0 45.7 %copy.45 = bf16[2,2,2,256,4608]{3,2,4,1,0:T(2,128)(2,1)} copy(bf16[2,2,2,256,4608]{4,3,2,1,0:T(8,128)(2,1)} %param.11) | data formatting | bytes 37748736 | tf_op args[0]
  55.7 45.4 %copy.46 = bf16[2,2,2,256,256,18]{4,3,5,2,1,0:T(8,128)(2,1)} copy(bf16[2,2,2,256,256,18]{3,2,5,4,1,0:T(2,128)(2,1)} %bitcast.68) | data formatting | bytes 37748736 | tf_op jit(solution)/shard_map/reshape | solution.py:78
  101.1 9.1 %slice.35 = bf16[2,1,2,256,256,18]{3,2,5,4,1,0:T(2,128)(2,1)} slice(bf16[2,2,2,256,256,18]{3,2,5,4,1,0:T(2,128)(2,1)} %bitcast.69), slice={[0:2], [0:1], [0:2], [0:256], [0:256], [0:18]} | slice | bytes 18874368 | tf_op jit(solution)/shard_map/slice | solution.py:84
  110.3 16.7 %broadcast_multiply_fusion.2 = bf16[2,2,2,256,256,18]{4,3,5,2,1,0:T(8,128)(2,1)} fusion(bf16[2,2,2,256,256,18]{4,3,5,2,1,0:T(8,128)(2,1)} %copy.46, bf16[2,2,256]{2,1,0:T(2,128)(2,1)S(1)} %compare_convert_fusion), kind=kLoop, calls=%fused_computation.84 | loop fusion | flops 9437184 | bytes 37750784 | tf_op jit(solution)/shard_map/mul | solution.py:79
  127.0 8.4 %slice_bitcast_fusion = bf16[2,2,256,256,18]{3,2,4,1,0:T(8,128)(2,1)} fusion(bf16[2,2,2,256,256,18]{4,3,5,2,1,0:T(8,128)(2,1)} %broadcast_multiply_fusion.2), kind=kLoop, calls=%fused_computation.83 | loop fusion | bytes 18874368 | tf_op jit(solution)/shard_map/squeeze | solution.py:84
  135.4 29.6 %copy.62 = bf16[2,2,2,256,256,18]{3,5,1,2,0,4:T(8,128)(2,1)} copy(bf16[2,2,2,256,256,18]{4,3,5,2,1,0:T(8,128)(2,1)} %broadcast_multiply_fusion.2) | data formatting | bytes 37748736 | tf_op jit(solution)/shard_map/mul | solution.py:79
  165.1 15.5 %copy.50 = bf16[2,2,256,256,18]{2,4,3,1,0:T(8,128)(2,1)} copy(bf16[2,2,256,256,18]{3,2,4,1,0:T(8,128)(2,1)} %slice_bitcast_fusion) | data formatting | bytes 18874368 | tf_op jit(solution)/shard_map/squeeze | solution.py:84
  180.6 13.3 %fusion.40 = f32[2,2,256,18,18]{4,3,2,1,0:T(8,128)} fusion(bf16[2,2,256,256,18]{2,4,3,1,0:T(8,128)(2,1)} %copy.50, bf16[2,1,2,256,256,18]{3,2,5,4,1,0:T(2,128)(2,1)} %slice.35), kind=kOutput, calls=%fused_computation.80 | convolution fusion | flops 169869312 | bytes 20201472 | tf_op jit(solution)/shard_map/skbai,skbaj->skaij/dot_general | solution.py:83
  193.9 14.0 %copy.51 = f32[2,2,256,18,18]{3,4,2,1,0:T(8,128)} copy(f32[2,2,256,18,18]{4,3,2,1,0:T(8,128)} %fusion.40) | data formatting | bytes 2654208 | tf_op jit(solution)/shard_map/skbai,skbaj->skaij/dot_general | solution.py:83
  207.9 14.1 %fusion.41 = f32[2,1,2,256,18,18]{5,4,3,2,0,1:T(8,128)} fusion(f32[2,2,256,18,18]{4,3,2,1,0:T(8,128)} %fusion.40, f32[2,2,256,18,18]{3,4,2,1,0:T(8,128)} %copy.51), kind=kLoop, calls=%fused_computation.82 | loop fusion | flops 331776 | bytes 3981312 | tf_op jit(solution)/shard_map/stack | solution.py:87
  221.9 11.4 %copy.53 = f32[2,1,2,256,18,18]{3,2,5,4,1,0:T(2,128)S(1)} copy(f32[2,1,2,256,18,18]{5,4,3,2,0,1:T(8,128)} %fusion.41) | data formatting | bytes 2654208 | tf_op jit(solution)/shard_map/stack | solution.py:87
  233.4 21.8 %fusion.42 = f32[2,1,2,256,18,18]{4,5,2,0,3,1:T(8,128)} fusion(bf16[2,2,2,256,256,18]{3,5,1,2,0,4:T(8,128)(2,1)} %copy.62, bf16[2,2,2,256,256,18]{3,2,5,4,1,0:T(2,128)(2,1)} %bitcast.70), kind=kOutput, calls=%fused_computation.85 | convolution fusion | flops 339738624 | bytes 39075840 | tf_op jit(solution)/shard_map/sckbai,sckbaj->skaij/dot_general | solution.py:80
  255.1 11.6 %copy.52 = f32[2,1,2,256,18,18]{3,2,5,4,1,0:T(2,128)S(1)} copy(f32[2,1,2,256,18,18]{4,5,2,0,3,1:T(8,128)} %fusion.42) | data formatting | bytes 2654208 | tf_op jit(solution)/shard_map/stack | solution.py:87
  266.8 3.7 fusion.45
  271.6 2.4 copy.56
  278.9 60.1 %all-reduce.2.cloned.1.call-done = f32[2,2,256,324]{3,1,2,0:T(2,128)} async-done(((f32[2,2,256,324]{3,1,2,0:T(2,128)}), f32[2,2,256,324]{3,1,2,0:T(2,128)}) %all-reduce.2.cloned.1.call-update) | async-done | bytes 1327120 | tf_op jit(solution)/shard_map/psum | solution.py:93
  339.0 2.2 gather_fusion
  342.3 4.4 all-gather
  346.8 303.3 %while.14 = (s32[]{:T(128)}, f32[64,3]{0,1:T(4,128)}, f32[2,1]{0,1:T(1,128)S(1)}, s32[8]{0:T(128)S(1)}, s32[]{:T(128)}, /*index=5*/f32[64,18]{0,1:T(8,128)S(1)},...) while((s32[]{:T(128)}, f32[64,3]{0,1:T(4,128)}, ...), condition=%wide.region_5.6_spmd.clone, body=%wide.region_4.5_spmd.clone.sunk | while | flops 262103424 | bytes 21960220 | solution.py:59
  351.1 1.2 add_subtract_fusion.2
  356.1 3.7 fusion.77
  359.8 1.3 dynamic-slice_reduce_fusion.3
  361.2 18.2 %convolution_multiply_fusion.3 = f32[13824,64]{0,1:T(8,128)} fusion(f32[18,13824]{1,0:T(8,128)} %mul.712, f32[64,18]{0,1:T(8,128)S(1)} %get-tuple-element.353, f32[13824,64]{0,1:T(8,128)S(1)} %fusion.77, f32[13824]{0:T(1024)S(1)} %get-tuple-element.318, f32[13824]{0:T(1024)S(1)} %get-tuple-element.319), kind=kOutput, calls=%fused_computation.3.clone.1 | convolution fusion | flops 194641920 | bytes 8188416 | tf_op jit(solution)/shard_map/while/body/eval_jaxpr/dot_general | solution.py:42
  379.4 5.5 convolution_add_fusion.2
  389.0 1.2 add_subtract_fusion.2
  394.0 3.7 fusion.77
  397.7 1.3 dynamic-slice_reduce_fusion.3
  399.1 18.2 %convolution_multiply_fusion.3 = f32[13824,64]{0,1:T(8,128)} fusion(f32[18,13824]{1,0:T(8,128)} %mul.712, f32[64,18]{0,1:T(8,128)S(1)} %get-tuple-element.353, f32[13824,64]{0,1:T(8,128)S(1)} %fusion.77, f32[13824]{0:T(1024)S(1)} %get-tuple-element.318, f32[13824]{0:T(1024)S(1)} %get-tuple-element.319), kind=kOutput, calls=%fused_computation.3.clone.1 | convolution fusion | flops 194641920 | bytes 8188416 | tf_op jit(solution)/shard_map/while/body/eval_jaxpr/dot_general | solution.py:42
  417.3 5.5 convolution_add_fusion.2
  426.9 1.2 add_subtract_fusion.2
  429.5 1.2 mul.712
  431.9 3.7 fusion.77
  435.6 1.3 dynamic-slice_reduce_fusion.3
  436.9 18.2 %convolution_multiply_fusion.3 = f32[13824,64]{0,1:T(8,128)} fusion(f32[18,13824]{1,0:T(8,128)} %mul.712, f32[64,18]{0,1:T(8,128)S(1)} %get-tuple-element.353, f32[13824,64]{0,1:T(8,128)S(1)} %fusion.77, f32[13824]{0:T(1024)S(1)} %get-tuple-element.318, f32[13824]{0:T(1024)S(1)} %get-tuple-element.319), kind=kOutput, calls=%fused_computation.3.clone.1 | convolution fusion | flops 194641920 | bytes 8188416 | tf_op jit(solution)/shard_map/while/body/eval_jaxpr/dot_general | solution.py:42
  455.2 5.5 convolution_add_fusion.2
  464.8 1.2 add_subtract_fusion.2
  467.4 1.2 mul.712
  469.8 3.7 fusion.77
  473.5 1.3 dynamic-slice_reduce_fusion.3
  474.8 18.2 %convolution_multiply_fusion.3 = f32[13824,64]{0,1:T(8,128)} fusion(f32[18,13824]{1,0:T(8,128)} %mul.712, f32[64,18]{0,1:T(8,128)S(1)} %get-tuple-element.353, f32[13824,64]{0,1:T(8,128)S(1)} %fusion.77, f32[13824]{0:T(1024)S(1)} %get-tuple-element.318, f32[13824]{0:T(1024)S(1)} %get-tuple-element.319), kind=kOutput, calls=%fused_computation.3.clone.1 | convolution fusion | flops 194641920 | bytes 8188416 | tf_op jit(solution)/shard_map/while/body/eval_jaxpr/dot_general | solution.py:42
  493.0 5.5 convolution_add_fusion.2
  502.7 1.2 add_subtract_fusion.2
  505.2 1.2 mul.712
  507.7 3.7 fusion.77
  511.4 1.3 dynamic-slice_reduce_fusion.3
  512.7 18.2 %convolution_multiply_fusion.3 = f32[13824,64]{0,1:T(8,128)} fusion(f32[18,13824]{1,0:T(8,128)} %mul.712, f32[64,18]{0,1:T(8,128)S(1)} %get-tuple-element.353, f32[13824,64]{0,1:T(8,128)S(1)} %fusion.77, f32[13824]{0:T(1024)S(1)} %get-tuple-element.318, f32[13824]{0:T(1024)S(1)} %get-tuple-element.319), kind=kOutput, calls=%fused_computation.3.clone.1 | convolution fusion | flops 194641920 | bytes 8188416 | tf_op jit(solution)/shard_map/while/body/eval_jaxpr/dot_general | solution.py:42
  530.9 5.5 convolution_add_fusion.2
  540.6 1.2 add_subtract_fusion.2
  545.6 3.7 fusion.77
  549.3 1.3 dynamic-slice_reduce_fusion.3
  550.6 18.2 %convolution_multiply_fusion.3 = f32[13824,64]{0,1:T(8,128)} fusion(f32[18,13824]{1,0:T(8,128)} %mul.712, f32[64,18]{0,1:T(8,128)S(1)} %get-tuple-element.353, f32[13824,64]{0,1:T(8,128)S(1)} %fusion.77, f32[13824]{0:T(1024)S(1)} %get-tuple-element.318, f32[13824]{0:T(1024)S(1)} %get-tuple-element.319), kind=kOutput, calls=%fused_computation.3.clone.1 | convolution fusion | flops 194641920 | bytes 8188416 | tf_op jit(solution)/shard_map/while/body/eval_jaxpr/dot_general | solution.py:42
  568.8 5.5 convolution_add_fusion.2
  578.5 1.2 add_subtract_fusion.2
  583.5 3.7 fusion.77
  587.2 1.3 dynamic-slice_reduce_fusion.3
  588.5 18.2 %convolution_multiply_fusion.3 = f32[13824,64]{0,1:T(8,128)} fusion(f32[18,13824]{1,0:T(8,128)} %mul.712, f32[64,18]{0,1:T(8,128)S(1)} %get-tuple-element.353, f32[13824,64]{0,1:T(8,128)S(1)} %fusion.77, f32[13824]{0:T(1024)S(1)} %get-tuple-element.318, f32[13824]{0:T(1024)S(1)} %get-tuple-element.319), kind=kOutput, calls=%fused_computation.3.clone.1 | convolution fusion | flops 194641920 | bytes 8188416 | tf_op jit(solution)/shard_map/while/body/eval_jaxpr/dot_general | solution.py:42
  606.7 5.5 convolution_add_fusion.2
  616.3 1.2 add_subtract_fusion.2
  621.4 3.7 fusion.77
  625.1 1.3 dynamic-slice_reduce_fusion.3
  626.4 18.2 %convolution_multiply_fusion.3 = f32[13824,64]{0,1:T(8,128)} fusion(f32[18,13824]{1,0:T(8,128)} %mul.712, f32[64,18]{0,1:T(8,128)S(1)} %get-tuple-element.353, f32[13824,64]{0,1:T(8,128)S(1)} %fusion.77, f32[13824]{0:T(1024)S(1)} %get-tuple-element.318, f32[13824]{0:T(1024)S(1)} %get-tuple-element.319), kind=kOutput, calls=%fused_computation.3.clone.1 | convolution fusion | flops 194641920 | bytes 8188416 | tf_op jit(solution)/shard_map/while/body/eval_jaxpr/dot_general | solution.py:42
  644.6 5.5 convolution_add_fusion.2
  650.2 4.9 psum.15
  (259 shorter events, 62.5 us)
Async XLA Ops:
  8.0 267.3 %copy-start = (s32[512]{0:T(512)S(1)}, s32[512]{0:T(512)}, u32[]{:S(2)}) copy-start(s32[512]{0:T(512)} %param.15) | copy-start | bytes 6148
  8.0 266.3 %sort.19.cloned.1.call-start = ((), (), s32[]{:S(2)}) async-start(), calls=%async_computation.1 | async-start | bytes 12320 | tf_op jit(solution)/shard_map/jit(argsort)/sort | solution.py:91
  9.9 329.0 %all-reduce.2.cloned.1.call-start = ((), (), s32[]{:S(2)}) async-start(), calls=%async_computation | async-start | bytes 3145728 | tf_op jit(solution)/shard_map/psum | solution.py:93
  101.1 9.1 %copy-start.8 = (s32[2,2]{1,0:T(2,128)S(1)}, s32[2,2]{1,0:T(2,128)}, u32[]{:S(2)}) copy-start(s32[2,2]{1,0:T(2,128)} %param.12) | copy-start | bytes 52
  255.1 11.6 %copy-start.9 = (f32[2]{0:T(128)S(1)}, f32[2]{0:T(128)}, u32[]{:S(2)}) copy-start(f32[2]{0:T(128)} %param.13) | copy-start | bytes 28
  270.5 3.6 copy-start.10
  270.5 3.6 copy-start.4
  270.6 3.6 copy-start.7
  347.0 1.2 copy-start.11
  347.0 6.4 copy-start.5
  355.3 0.8 copy-start.1
  356.1 3.7 copy-start.2
  356.1 3.7 copy-start.3
  379.4 5.5 copy-start.6
  379.4 5.5 copy-start.12
  384.9 1.2 copy-start.11
  384.9 6.4 copy-start.5
  393.2 0.8 copy-start.1
  394.0 3.7 copy-start.2
  394.0 3.7 copy-start.3
  417.3 5.5 copy-start.6
  417.3 5.5 copy-start.12
  422.8 1.2 copy-start.11
  422.8 6.4 copy-start.5
  431.0 0.8 copy-start.1
  431.9 3.7 copy-start.2
  431.9 3.7 copy-start.3
  455.2 5.5 copy-start.6
  455.2 5.5 copy-start.12
  460.7 1.2 copy-start.11
  460.7 6.4 copy-start.5
  468.9 0.8 copy-start.1
  469.8 3.7 copy-start.2
  469.8 3.7 copy-start.3
  493.0 5.5 copy-start.6
  493.0 5.5 copy-start.12
  498.6 1.2 copy-start.11
  498.6 6.4 copy-start.5
  506.8 0.8 copy-start.1
  507.7 3.7 copy-start.2
  507.7 3.7 copy-start.3
  530.9 5.5 copy-start.6
  530.9 5.5 copy-start.12
  536.5 1.2 copy-start.11
  536.5 6.4 copy-start.5
  544.7 0.8 copy-start.1
  545.6 3.7 copy-start.2
  545.6 3.7 copy-start.3
  568.8 5.5 copy-start.6
  568.8 5.5 copy-start.12
  574.4 1.2 copy-start.11
  574.4 6.4 copy-start.5
  582.6 0.8 copy-start.1
  583.5 3.7 copy-start.2
  583.5 3.7 copy-start.3
  606.7 5.5 copy-start.6
  606.7 5.5 copy-start.12
  612.3 1.2 copy-start.11
  612.3 6.4 copy-start.5
  620.5 0.8 copy-start.1
  621.3 3.7 copy-start.2
  621.4 3.7 copy-start.3
  644.6 5.5 copy-start.6
  644.6 5.5 copy-start.12
Sparse Core Ops, SparseCore 0:
  11.7 2.2 sort.21.cloned.1.call-done
  (1 shorter events, 0.0 us)
Sparse Core Ops, SparseCore 1:
  274.1 64.8 all-reduce.1
where the time goes:
time: 668 us; the launch traced here: 663 us
  matrix products  255 us (38%)
  local copies, waits for them, and re-layouts  234 us (35%)
  other arithmetic  83.3 us (12%)
  waiting for transfers between devices  60.1 us (9%)
  between operations  15.7 us (2%)
  blocking collectives  9.31 us (1%)
    dot_general x8, matrix products, force_block(): smooth = jnp.dot(moments, form_table, precision=highest)  146 us
    psum x1, waiting for transfers between devices, shards(): summed = lax.psum(density_local, ('ka', 'ba'))  60.1 us
    unnamed x19, local copies, waits for them, and re-layouts  47.3 us
    reshape x1, local copies, waits for them, and re-layouts, shards(): coefficients.reshape(spin_count, complex_parts, kcount, bcount, atoms_blk...  45.4 us
    dot_general x8, matrix products, force_block(): return jnp.dot(smooth * wave_term, vectors, precision=highest)  44.3 us
    mul x1, local copies, waits for them, and re-layouts, shards(): masked = values * band_mask[:, None, :, :, None, None]  29.6 us
    dot_general x8, matrix products, force_block(): phases = jnp.dot(places, vectors.T, precision=highest)  29.6 us
    squeeze x2, local copies, waits for them, and re-layouts, shards(): masked[:, 1]  23.9 us
  transfers between devices with their start and end apart: 1, of which 1 were waited for; matrix products, arithmetic and copies ran while one was open for 1% of the time, Pallas kernels for 0%

commit v1 on v0

--- a/solution.py
+++ b/solution.py
@@ -90,7 +90,7 @@
     )
     ranking = jnp.argsort(owner_map.reshape(-1, atoms_blk), axis=1, stable=True)
     own_ranks = lax.dynamic_slice_in_dim(ranking, owner_index * per_owner, per_owner, 1)
-    summed = lax.psum(density_local, ("ka", "ba"))
+    summed = lax.psum(lax.psum(density_local, "ka"), "ba")
     own_rows = lax.dynamic_index_in_dim(own_ranks, group_index, 0, keepdims=False)
     own_density = jnp.take(summed, own_rows, axis=2)
     block_count = own_ranks.shape[0]

time: 668 us -> 696 us (1.042)
  waiting for transfers between devices: 60.1 us -> 88.1 us
    psum x1 -> x2, waiting for transfers between devices: 60.1 us -> 88.1 us  [shards(): summed = lax.psum(lax.psum(density_local, 'ka'), 'ba')]
  transfers between devices with their start and end apart: 1 -> 2, of which waited for: 1 -> 2; matrix products, arithmetic and copies ran while one was open for 1% -> 1% of each run, Pallas kernels for 0% -> 0%
where the time goes in v1:
time: 696 us; the launch traced here: 691 us
  matrix products  255 us (37%)
  local copies, waits for them, and re-layouts  234 us (34%)
  waiting for transfers between devices  88.1 us (13%)
  other arithmetic  83.3 us (12%)
  between operations  15.8 us (2%)
  blocking collectives  9.31 us (1%)
    dot_general x8, matrix products, force_block(): smooth = jnp.dot(moments, form_table, precision=highest)  146 us
    psum x2, waiting for transfers between devices, shards(): summed = lax.psum(lax.psum(density_local, 'ka'), 'ba')  88.1 us
    unnamed x19, local copies, waits for them, and re-layouts  47.3 us
    reshape x1, local copies, waits for them, and re-layouts, shards(): coefficients.reshape(spin_count, complex_parts, kcount, bcount, atoms_blk...  45.4 us
    dot_general x8, matrix products, force_block(): return jnp.dot(smooth * wave_term, vectors, precision=highest)  44.3 us
    mul x1, local copies, waits for them, and re-layouts, shards(): masked = values * band_mask[:, None, :, :, None, None]  29.6 us
    dot_general x8, matrix products, force_block(): phases = jnp.dot(places, vectors.T, precision=highest)  29.6 us
    squeeze x2, local copies, waits for them, and re-layouts, shards(): masked[:, 1]  23.9 us
  transfers between devices with their start and end apart: 2, of which 2 were waited for; matrix products, arithmetic and copies ran while one was open for 1% of the time, Pallas kernels for 0%

profile of v1, /device:TPU:0, one launch (start us, length us, event | category | flops | bytes accessed | tf_op | source)
XLA Modules:
  0.0 691.2 jit_solution(6792068242337037878)
XLA Ops:
  8.1 1.3 reshape.503
  10.0 45.7 %copy.45 = bf16[2,2,2,256,4608]{3,2,4,1,0:T(2,128)(2,1)} copy(bf16[2,2,2,256,4608]{4,3,2,1,0:T(8,128)(2,1)} %param.11) | data formatting | bytes 37748736 | tf_op args[0]
  55.7 45.4 %copy.46 = bf16[2,2,2,256,256,18]{4,3,5,2,1,0:T(8,128)(2,1)} copy(bf16[2,2,2,256,256,18]{3,2,5,4,1,0:T(2,128)(2,1)} %bitcast.68) | data formatting | bytes 37748736 | tf_op jit(solution)/shard_map/reshape | solution.py:78
  101.1 9.1 %slice.35 = bf16[2,1,2,256,256,18]{3,2,5,4,1,0:T(2,128)(2,1)} slice(bf16[2,2,2,256,256,18]{3,2,5,4,1,0:T(2,128)(2,1)} %bitcast.69), slice={[0:2], [0:1], [0:2], [0:256], [0:256], [0:18]} | slice | bytes 18874368 | tf_op jit(solution)/shard_map/slice | solution.py:84
  110.3 16.7 %broadcast_multiply_fusion.2 = bf16[2,2,2,256,256,18]{4,3,5,2,1,0:T(8,128)(2,1)} fusion(bf16[2,2,2,256,256,18]{4,3,5,2,1,0:T(8,128)(2,1)} %copy.46, bf16[2,2,256]{2,1,0:T(2,128)(2,1)S(1)} %compare_convert_fusion), kind=kLoop, calls=%fused_computation.84 | loop fusion | flops 9437184 | bytes 37750784 | tf_op jit(solution)/shard_map/mul | solution.py:79
  127.0 8.4 %slice_bitcast_fusion = bf16[2,2,256,256,18]{3,2,4,1,0:T(8,128)(2,1)} fusion(bf16[2,2,2,256,256,18]{4,3,5,2,1,0:T(8,128)(2,1)} %broadcast_multiply_fusion.2), kind=kLoop, calls=%fused_computation.83 | loop fusion | bytes 18874368 | tf_op jit(solution)/shard_map/squeeze | solution.py:84
  135.4 29.6 %copy.62 = bf16[2,2,2,256,256,18]{3,5,1,2,0,4:T(8,128)(2,1)} copy(bf16[2,2,2,256,256,18]{4,3,5,2,1,0:T(8,128)(2,1)} %broadcast_multiply_fusion.2) | data formatting | bytes 37748736 | tf_op jit(solution)/shard_map/mul | solution.py:79
  165.1 15.5 %copy.50 = bf16[2,2,256,256,18]{2,4,3,1,0:T(8,128)(2,1)} copy(bf16[2,2,256,256,18]{3,2,4,1,0:T(8,128)(2,1)} %slice_bitcast_fusion) | data formatting | bytes 18874368 | tf_op jit(solution)/shard_map/squeeze | solution.py:84
  180.6 13.3 %fusion.40 = f32[2,2,256,18,18]{4,3,2,1,0:T(8,128)} fusion(bf16[2,2,256,256,18]{2,4,3,1,0:T(8,128)(2,1)} %copy.50, bf16[2,1,2,256,256,18]{3,2,5,4,1,0:T(2,128)(2,1)} %slice.35), kind=kOutput, calls=%fused_computation.80 | convolution fusion | flops 169869312 | bytes 20201472 | tf_op jit(solution)/shard_map/skbai,skbaj->skaij/dot_general | solution.py:83
  193.9 14.0 %copy.51 = f32[2,2,256,18,18]{3,4,2,1,0:T(8,128)} copy(f32[2,2,256,18,18]{4,3,2,1,0:T(8,128)} %fusion.40) | data formatting | bytes 2654208 | tf_op jit(solution)/shard_map/skbai,skbaj->skaij/dot_general | solution.py:83
  207.9 14.1 %fusion.41 = f32[2,1,2,256,18,18]{5,4,3,2,0,1:T(8,128)} fusion(f32[2,2,256,18,18]{4,3,2,1,0:T(8,128)} %fusion.40, f32[2,2,256,18,18]{3,4,2,1,0:T(8,128)} %copy.51), kind=kLoop, calls=%fused_computation.82 | loop fusion | flops 331776 | bytes 3981312 | tf_op jit(solution)/shard_map/stack | solution.py:87
  221.9 11.4 %copy.53 = f32[2,1,2,256,18,18]{3,2,5,4,1,0:T(2,128)S(1)} copy(f32[2,1,2,256,18,18]{5,4,3,2,0,1:T(8,128)} %fusion.41) | data formatting | bytes 2654208 | tf_op jit(solution)/shard_map/stack | solution.py:87
  233.4 21.8 %fusion.42 = f32[2,1,2,256,18,18]{4,5,2,0,3,1:T(8,128)} fusion(bf16[2,2,2,256,256,18]{3,5,1,2,0,4:T(8,128)(2,1)} %copy.62, bf16[2,2,2,256,256,18]{3,2,5,4,1,0:T(2,128)(2,1)} %bitcast.70), kind=kOutput, calls=%fused_computation.85 | convolution fusion | flops 339738624 | bytes 39075840 | tf_op jit(solution)/shard_map/sckbai,sckbaj->skaij/dot_general | solution.py:80
  255.1 11.6 %copy.52 = f32[2,1,2,256,18,18]{3,2,5,4,1,0:T(2,128)S(1)} copy(f32[2,1,2,256,18,18]{4,5,2,0,3,1:T(8,128)} %fusion.42) | data formatting | bytes 2654208 | tf_op jit(solution)/shard_map/stack | solution.py:87
  266.8 3.7 fusion.45
  271.6 2.4 copy.56
  276.1 69.6 %all-reduce.3.cloned.1.call-done = f32[2,2,256,324]{3,1,2,0:T(2,128)} async-done(((f32[2,2,256,324]{3,1,2,0:T(2,128)}), f32[2,2,256,324]{3,1,2,0:T(2,128)}) %all-reduce.3.cloned.1.call-update) | async-done | bytes 1327120 | tf_op jit(solution)/shard_map/psum | solution.py:93
  348.6 18.5 %all-reduce.5.cloned.1.call-done = f32[2,2,256,324]{3,1,2,0:T(2,128)} async-done(((f32[2,2,256,324]{3,1,2,0:T(2,128)}), f32[2,2,256,324]{3,1,2,0:T(2,128)}) %all-reduce.5.cloned.1.call-update) | async-done | bytes 1327120 | tf_op jit(solution)/shard_map/psum | solution.py:93
  367.1 2.2 gather_fusion
  370.5 4.4 all-gather
  374.9 303.2 %while.14 = (s32[]{:T(128)}, f32[64,3]{0,1:T(4,128)}, f32[2,1]{0,1:T(1,128)S(1)}, s32[8]{0:T(128)S(1)}, s32[]{:T(128)}, /*index=5*/f32[64,18]{0,1:T(8,128)S(1)},...) while((s32[]{:T(128)}, f32[64,3]{0,1:T(4,128)}, ...), condition=%wide.region_6.7_spmd.clone, body=%wide.region_5.6_spmd.clone.sunk | while | flops 262103424 | bytes 21960220 | solution.py:59
  379.2 1.2 add_subtract_fusion.2
  384.2 3.7 fusion.77
  387.9 1.3 dynamic-slice_reduce_fusion.3
  389.3 18.2 %convolution_multiply_fusion.3 = f32[13824,64]{0,1:T(8,128)} fusion(f32[18,13824]{1,0:T(8,128)} %mul.712, f32[64,18]{0,1:T(8,128)S(1)} %get-tuple-element.353, f32[13824,64]{0,1:T(8,128)S(1)} %fusion.77, f32[13824]{0:T(1024)S(1)} %get-tuple-element.318, f32[13824]{0:T(1024)S(1)} %get-tuple-element.319), kind=kOutput, calls=%fused_computation.3.clone.1 | convolution fusion | flops 194641920 | bytes 8188416 | tf_op jit(solution)/shard_map/while/body/eval_jaxpr/dot_general | solution.py:42
  407.5 5.5 convolution_add_fusion.2
  417.1 1.2 add_subtract_fusion.2
  419.6 1.2 mul.712
  422.1 3.7 fusion.77
  425.8 1.3 dynamic-slice_reduce_fusion.3
  427.1 18.2 %convolution_multiply_fusion.3 = f32[13824,64]{0,1:T(8,128)} fusion(f32[18,13824]{1,0:T(8,128)} %mul.712, f32[64,18]{0,1:T(8,128)S(1)} %get-tuple-element.353, f32[13824,64]{0,1:T(8,128)S(1)} %fusion.77, f32[13824]{0:T(1024)S(1)} %get-tuple-element.318, f32[13824]{0:T(1024)S(1)} %get-tuple-element.319), kind=kOutput, calls=%fused_computation.3.clone.1 | convolution fusion | flops 194641920 | bytes 8188416 | tf_op jit(solution)/shard_map/while/body/eval_jaxpr/dot_general | solution.py:42
  445.3 5.5 convolution_add_fusion.2
  454.9 1.2 add_subtract_fusion.2
  460.0 3.7 fusion.77
  463.7 1.3 dynamic-slice_reduce_fusion.3
  465.0 18.2 %convolution_multiply_fusion.3 = f32[13824,64]{0,1:T(8,128)} fusion(f32[18,13824]{1,0:T(8,128)} %mul.712, f32[64,18]{0,1:T(8,128)S(1)} %get-tuple-element.353, f32[13824,64]{0,1:T(8,128)S(1)} %fusion.77, f32[13824]{0:T(1024)S(1)} %get-tuple-element.318, f32[13824]{0:T(1024)S(1)} %get-tuple-element.319), kind=kOutput, calls=%fused_computation.3.clone.1 | convolution fusion | flops 194641920 | bytes 8188416 | tf_op jit(solution)/shard_map/while/body/eval_jaxpr/dot_general | solution.py:42
  483.2 5.5 convolution_add_fusion.2
  492.8 1.2 add_subtract_fusion.2
  497.9 3.7 fusion.77
  501.6 1.3 dynamic-slice_reduce_fusion.3
  502.9 18.2 %convolution_multiply_fusion.3 = f32[13824,64]{0,1:T(8,128)} fusion(f32[18,13824]{1,0:T(8,128)} %mul.712, f32[64,18]{0,1:T(8,128)S(1)} %get-tuple-element.353, f32[13824,64]{0,1:T(8,128)S(1)} %fusion.77, f32[13824]{0:T(1024)S(1)} %get-tuple-element.318, f32[13824]{0:T(1024)S(1)} %get-tuple-element.319), kind=kOutput, calls=%fused_computation.3.clone.1 | convolution fusion | flops 194641920 | bytes 8188416 | tf_op jit(solution)/shard_map/while/body/eval_jaxpr/dot_general | solution.py:42
  521.1 5.5 convolution_add_fusion.2
  530.7 1.2 add_subtract_fusion.2
  533.3 1.2 mul.712
  535.7 3.7 fusion.77
  539.5 1.3 dynamic-slice_reduce_fusion.3
  540.8 18.2 %convolution_multiply_fusion.3 = f32[13824,64]{0,1:T(8,128)} fusion(f32[18,13824]{1,0:T(8,128)} %mul.712, f32[64,18]{0,1:T(8,128)S(1)} %get-tuple-element.353, f32[13824,64]{0,1:T(8,128)S(1)} %fusion.77, f32[13824]{0:T(1024)S(1)} %get-tuple-element.318, f32[13824]{0:T(1024)S(1)} %get-tuple-element.319), kind=kOutput, calls=%fused_computation.3.clone.1 | convolution fusion | flops 194641920 | bytes 8188416 | tf_op jit(solution)/shard_map/while/body/eval_jaxpr/dot_general | solution.py:42
  559.0 5.5 convolution_add_fusion.2
  568.6 1.2 add_subtract_fusion.2
  573.6 3.7 fusion.77
  577.3 1.3 dynamic-slice_reduce_fusion.3
  578.7 18.2 %convolution_multiply_fusion.3 = f32[13824,64]{0,1:T(8,128)} fusion(f32[18,13824]{1,0:T(8,128)} %mul.712, f32[64,18]{0,1:T(8,128)S(1)} %get-tuple-element.353, f32[13824,64]{0,1:T(8,128)S(1)} %fusion.77, f32[13824]{0:T(1024)S(1)} %get-tuple-element.318, f32[13824]{0:T(1024)S(1)} %get-tuple-element.319), kind=kOutput, calls=%fused_computation.3.clone.1 | convolution fusion | flops 194641920 | bytes 8188416 | tf_op jit(solution)/shard_map/while/body/eval_jaxpr/dot_general | solution.py:42
  596.9 5.5 convolution_add_fusion.2
  606.5 1.2 add_subtract_fusion.2
  611.5 3.7 fusion.77
  615.2 1.3 dynamic-slice_reduce_fusion.3
  616.5 18.2 %convolution_multiply_fusion.3 = f32[13824,64]{0,1:T(8,128)} fusion(f32[18,13824]{1,0:T(8,128)} %mul.712, f32[64,18]{0,1:T(8,128)S(1)} %get-tuple-element.353, f32[13824,64]{0,1:T(8,128)S(1)} %fusion.77, f32[13824]{0:T(1024)S(1)} %get-tuple-element.318, f32[13824]{0:T(1024)S(1)} %get-tuple-element.319), kind=kOutput, calls=%fused_computation.3.clone.1 | convolution fusion | flops 194641920 | bytes 8188416 | tf_op jit(solution)/shard_map/while/body/eval_jaxpr/dot_general | solution.py:42
  634.7 5.5 convolution_add_fusion.2
  644.3 1.2 add_subtract_fusion.2
  649.4 3.7 fusion.77
  653.1 1.3 dynamic-slice_reduce_fusion.3
  654.4 18.2 %convolution_multiply_fusion.3 = f32[13824,64]{0,1:T(8,128)} fusion(f32[18,13824]{1,0:T(8,128)} %mul.712, f32[64,18]{0,1:T(8,128)S(1)} %get-tuple-element.353, f32[13824,64]{0,1:T(8,128)S(1)} %fusion.77, f32[13824]{0:T(1024)S(1)} %get-tuple-element.318, f32[13824]{0:T(1024)S(1)} %get-tuple-element.319), kind=kOutput, calls=%fused_computation.3.clone.1 | convolution fusion | flops 194641920 | bytes 8188416 | tf_op jit(solution)/shard_map/while/body/eval_jaxpr/dot_general | solution.py:42
  672.6 5.5 convolution_add_fusion.2
  678.2 4.9 psum.23
  (262 shorter events, 63.8 us)
Async XLA Ops:
  8.0 267.3 %copy-start = (s32[512]{0:T(512)S(1)}, s32[512]{0:T(512)}, u32[]{:S(2)}) copy-start(s32[512]{0:T(512)} %param.15) | copy-start | bytes 6148
  8.0 266.4 %sort.19.cloned.1.call-start = ((), (), s32[]{:S(2)}) async-start(), calls=%async_computation.2 | async-start | bytes 12320 | tf_op jit(solution)/shard_map/jit(argsort)/sort | solution.py:91
  9.9 335.7 %all-reduce.3.cloned.1.call-start = ((), (), s32[]{:S(2)}) async-start(), calls=%async_computation | async-start | bytes 3145728 | tf_op jit(solution)/shard_map/psum | solution.py:93
  101.1 9.1 %copy-start.8 = (s32[2,2]{1,0:T(2,128)S(1)}, s32[2,2]{1,0:T(2,128)}, u32[]{:S(2)}) copy-start(s32[2,2]{1,0:T(2,128)} %param.12) | copy-start | bytes 52
  255.1 11.6 %copy-start.9 = (f32[2]{0:T(128)S(1)}, f32[2]{0:T(128)}, u32[]{:S(2)}) copy-start(f32[2]{0:T(128)} %param.13) | copy-start | bytes 28
  270.5 3.6 copy-start.4
  270.5 3.6 copy-start.7
  270.6 3.8 copy-start.10
  274.1 93.0 %all-reduce.5.cloned.1.call-start = ((), (), s32[]{:S(2)}) async-start(), calls=%async_computation.1 | async-start | bytes 3145728 | tf_op jit(solution)/shard_map/psum | solution.py:93
  375.1 7.8 %copy-start.5 = (f32[2,1]{0,1:T(1,128)}, f32[2,1]{0,1:T(1,128)S(1)}, u32[]{:S(2)}) copy-start(f32[2,1]{0,1:T(1,128)S(1)} %get-tuple-element.350) | copy-start | bytes 28 | tf_op jit(solution)/shard_map/while
  375.1 7.8 %copy-start.11 = (s32[8]{0:T(128)}, s32[8]{0:T(128)S(1)}, u32[]{:S(2)}) copy-start(s32[8]{0:T(128)S(1)} %get-tuple-element.351) | copy-start | bytes 100 | tf_op jit(solution)/shard_map/while
  383.4 0.8 copy-start.1
  384.2 3.7 copy-start.2
  384.2 3.7 copy-start.3
  407.5 5.5 copy-start.6
  407.5 5.5 copy-start.12
  413.0 7.8 %copy-start.5 = (f32[2,1]{0,1:T(1,128)}, f32[2,1]{0,1:T(1,128)S(1)}, u32[]{:S(2)}) copy-start(f32[2,1]{0,1:T(1,128)S(1)} %get-tuple-element.350) | copy-start | bytes 28 | tf_op jit(solution)/shard_map/while
  413.0 7.8 %copy-start.11 = (s32[8]{0:T(128)}, s32[8]{0:T(128)S(1)}, u32[]{:S(2)}) copy-start(s32[8]{0:T(128)S(1)} %get-tuple-element.351) | copy-start | bytes 100 | tf_op jit(solution)/shard_map/while
  421.2 0.8 copy-start.1
  422.1 3.7 copy-start.2
  422.1 3.7 copy-start.3
  445.3 5.5 copy-start.6
  445.3 5.5 copy-start.12
  450.9 7.8 %copy-start.5 = (f32[2,1]{0,1:T(1,128)}, f32[2,1]{0,1:T(1,128)S(1)}, u32[]{:S(2)}) copy-start(f32[2,1]{0,1:T(1,128)S(1)} %get-tuple-element.350) | copy-start | bytes 28 | tf_op jit(solution)/shard_map/while
  450.9 7.8 %copy-start.11 = (s32[8]{0:T(128)}, s32[8]{0:T(128)S(1)}, u32[]{:S(2)}) copy-start(s32[8]{0:T(128)S(1)} %get-tuple-element.351) | copy-start | bytes 100 | tf_op jit(solution)/shard_map/while
  459.1 0.8 copy-start.1
  459.9 3.7 copy-start.2
  460.0 3.7 copy-start.3
  483.2 5.5 copy-start.6
  483.2 5.5 copy-start.12
  488.8 7.8 %copy-start.5 = (f32[2,1]{0,1:T(1,128)}, f32[2,1]{0,1:T(1,128)S(1)}, u32[]{:S(2)}) copy-start(f32[2,1]{0,1:T(1,128)S(1)} %get-tuple-element.350) | copy-start | bytes 28 | tf_op jit(solution)/shard_map/while
  488.8 7.8 %copy-start.11 = (s32[8]{0:T(128)}, s32[8]{0:T(128)S(1)}, u32[]{:S(2)}) copy-start(s32[8]{0:T(128)S(1)} %get-tuple-element.351) | copy-start | bytes 100 | tf_op jit(solution)/shard_map/while
  497.0 0.8 copy-start.1
  497.8 3.7 copy-start.2
  497.8 3.7 copy-start.3
  521.1 5.5 copy-start.6
  521.1 5.5 copy-start.12
  526.6 7.8 %copy-start.5 = (f32[2,1]{0,1:T(1,128)}, f32[2,1]{0,1:T(1,128)S(1)}, u32[]{:S(2)}) copy-start(f32[2,1]{0,1:T(1,128)S(1)} %get-tuple-element.350) | copy-start | bytes 28 | tf_op jit(solution)/shard_map/while
  526.6 7.8 %copy-start.11 = (s32[8]{0:T(128)}, s32[8]{0:T(128)S(1)}, u32[]{:S(2)}) copy-start(s32[8]{0:T(128)S(1)} %get-tuple-element.351) | copy-start | bytes 100 | tf_op jit(solution)/shard_map/while
  534.9 0.8 copy-start.1
  535.7 3.7 copy-start.2
  535.7 3.7 copy-start.3
  559.0 5.5 copy-start.6
  559.0 5.5 copy-start.12
  564.5 7.8 %copy-start.5 = (f32[2,1]{0,1:T(1,128)}, f32[2,1]{0,1:T(1,128)S(1)}, u32[]{:S(2)}) copy-start(f32[2,1]{0,1:T(1,128)S(1)} %get-tuple-element.350) | copy-start | bytes 28 | tf_op jit(solution)/shard_map/while
  564.5 7.8 %copy-start.11 = (s32[8]{0:T(128)}, s32[8]{0:T(128)S(1)}, u32[]{:S(2)}) copy-start(s32[8]{0:T(128)S(1)} %get-tuple-element.351) | copy-start | bytes 100 | tf_op jit(solution)/shard_map/while
  572.8 0.8 copy-start.1
  573.6 3.7 copy-start.2
  573.6 3.7 copy-start.3
  596.9 5.5 copy-start.6
  596.9 5.5 copy-start.12
  602.4 7.8 %copy-start.5 = (f32[2,1]{0,1:T(1,128)}, f32[2,1]{0,1:T(1,128)S(1)}, u32[]{:S(2)}) copy-start(f32[2,1]{0,1:T(1,128)S(1)} %get-tuple-element.350) | copy-start | bytes 28 | tf_op jit(solution)/shard_map/while
  602.4 7.8 %copy-start.11 = (s32[8]{0:T(128)}, s32[8]{0:T(128)S(1)}, u32[]{:S(2)}) copy-start(s32[8]{0:T(128)S(1)} %get-tuple-element.351) | copy-start | bytes 100 | tf_op jit(solution)/shard_map/while
  611.5 3.7 copy-start.2
  611.5 3.7 copy-start.3
  634.7 5.5 copy-start.6
  634.7 5.5 copy-start.12
  640.3 7.8 %copy-start.5 = (f32[2,1]{0,1:T(1,128)}, f32[2,1]{0,1:T(1,128)S(1)}, u32[]{:S(2)}) copy-start(f32[2,1]{0,1:T(1,128)S(1)} %get-tuple-element.350) | copy-start | bytes 28 | tf_op jit(solution)/shard_map/while
  640.3 7.8 %copy-start.11 = (s32[8]{0:T(128)}, s32[8]{0:T(128)S(1)}, u32[]{:S(2)}) copy-start(s32[8]{0:T(128)S(1)} %get-tuple-element.351) | copy-start | bytes 100 | tf_op jit(solution)/shard_map/while
  648.5 0.8 copy-start.1
  649.3 3.7 copy-start.2
  649.3 3.7 copy-start.3
  672.6 5.5 copy-start.6
  672.6 5.5 copy-start.12
  (1 other events, 0.8 us)
Sparse Core Ops, SparseCore 0:
  11.7 2.2 sort.21.cloned.1.call-done
  (1 shorter events, 0.0 us)
Sparse Core Ops, SparseCore 1:
  274.1 71.4 all-reduce.2
  347.8 19.2 all-reduce.4
